TPU v7x, 32 devices: a whole 2x2x4 slice. The times are simulated.
32 devices in a mesh: group: 4 (over y, x), row: 8 (over z, core).
Axes of the slice: x: 2, y: 2, z: 4, core: 2. Of those that a mesh axis runs over, the one named last changes fastest.
Arguments:
- snapshots: bfloat16 [1024, 8192], P(('group', 'row')), may hold values from -6 to 6
- bnd_index: int32 [16, 1024], replicated, may hold values from 0 to 8191
- recovery: bfloat16 [512, 512, 1024], P(('group', 'row')), may hold values from -0.1875 to 0.1875
- block_se: int32 [512], P(('group', 'row')), may hold values from 0 to 3
- connect: int32 [16384, 24], P(('group', 'row')), may hold values from 0 to 8703, as said below
- stress_mat: bfloat16 [16384, 6, 24], P(('group', 'row')), may hold values from -1.25 to 1.25
Outputs:
- stresses: bfloat16 [16384, 6, 1024], P(('group', 'row'))
Inputs may be any that keep to these rules, and one draw needn't show every extreme that they name: `connect`: among one device's elements, the first 8192 entries of its connectivity, read element by element, name each of rows 256 to 8447 once.
All inputs are finite; a program needn't handle non-finite values.
Results may differ from a plain program's by a relative error of at most 0.0049.
Values may be sent and summed in bfloat16 or wider, within the bound.
No kernel may reach another device: no remote copies, remote signals or barrier semaphores. Data moves between devices by JAX's collectives and lax.ppermute only.
A program may use at most 128 MiB of HBM per device.

v0:
```python
import math
import jax
import jax.numpy as jnp
from jax import lax
from jax.sharding import PartitionSpec as P

HW = 256
NC = 6
NDOF = 24


def extended_2(cells, sides, width):
    for axis, dim in sides:
        count = lax.axis_size(axis)
        ends = count - 1
        head = lax.slice_in_dim(cells, 0, width, axis=dim)
        tail = lax.slice_in_dim(cells, cells.shape[dim] - width, cells.shape[dim], axis=dim)
        cells = jnp.concatenate(
            [
                lax.ppermute(tail, axis, [(i, (i + 1) % count) for i in range(ends)]),
                cells,
                lax.ppermute(head, axis, [((i + 1) % count, i) for i in range(ends)]),
            ],
            axis=dim,
        )
    return cells


def body(snapshots, bnd_index, recovery, block_se, connect, stress_mat):
    picked = jnp.take(snapshots, bnd_index, axis=1)
    widened = lax.all_gather(picked, "row", axis=0, tiled=True)
    arrived = lax.all_to_all(widened, "group", split_axis=1, concat_axis=0, tiled=True)
    bvals = jnp.transpose(arrived, (1, 0, 2))

    def one_block(entry):
        matrix, which = entry
        sliced = lax.dynamic_index_in_dim(bvals, which, 0, keepdims=False)
        result = lax.dot_general(
            matrix, sliced, (((1,), (1,)), ((), ())), preferred_element_type=jnp.float32
        )
        return result.astype(jnp.bfloat16)

    interior = lax.map(one_block, (recovery, block_se))
    interior = interior.reshape(interior.shape[0] * interior.shape[1], interior.shape[2])
    extended = extended_2(interior, (("row", 0),), HW)
    elem_count = connect.shape[0]
    elem_block = math.gcd(elem_count, 128)

    def one_part(entry):
        link_rows, mat_rows = entry
        values = jnp.take(extended, link_rows, axis=0)
        result = jnp.einsum("eck,ekt->ect", mat_rows, values, preferred_element_type=jnp.float32)
        return result.astype(jnp.bfloat16)

    links = connect.reshape(elem_count // elem_block, elem_block, NDOF)
    mats = stress_mat.reshape(elem_count // elem_block, elem_block, NC, NDOF)
    stresses = lax.map(one_part, (links, mats))
    return stresses.reshape(elem_count, NC, extended.shape[1])


def solution(mesh):
    in_specs = (
        P(("group", "row"), None),
        P(),
        P(("group", "row"), None, None),
        P(("group", "row")),
        P(("group", "row"), None),
        P(("group", "row"), None, None),
    )
    out_specs = P(("group", "row"), None, None)
    return jax.shard_map(body, mesh=mesh, in_specs=in_specs, out_specs=out_specs, check_vma=False)
```

profile of v0, /device:TPU:1, one launch (start us, length us, event | category | flops | bytes accessed | tf_op | source)
XLA Modules:
  0.0 552.2 jit_solution(11753239106156816748)
XLA Ops:
  6.5 0.8 fusion.25
  7.4 0.9 compare_and_fusion.1
  8.2 1.9 copy.25
  10.2 57.9 %gather_fusion.1 = bf16[16384,32]{1,0:T(8,128)(2,1)} fusion(bf16[32,8192]{0,1:T(8,128)(2,1)S(1)} %copy.25, s32[16384]{0:T(1024)S(1)} %broadcast_clamp_fusion.1), kind=kCustom, calls=%fused_computation.1 | custom fusion | bytes 2162688 | tf_op jit(solution)/shard_map/jit(_take)/gather | solution.py:30
  68.1 4.0 copy.26
  72.1 1.1 select_bitcast_fusion
  73.2 84.7 %all-gather.2.cloned.1.call-done = bf16[256,16,1024]{2,1,0:T(8,128)(2,1)} async-done(((bf16[32,16,1024]{2,1,0:T(8,128)(2,1)}), bf16[256,16,1024]{2,1,0:T(8,128)(2,1)}) %all-gather.2.cloned.1.call-update) | async-done | bytes 8388624 | tf_op jit(solution)/shard_map/all_gather | solution.py:31
  157.9 11.3 %copy.27 = bf16[256,16,1024]{2,0,1:T(8,128)(2,1)} copy(bf16[256,16,1024]{2,1,0:T(8,128)(2,1)} %all-gather.2.cloned.1.call-done) | data formatting | bytes 16777216 | tf_op jit(solution)/shard_map/all_gather | solution.py:31
  169.2 5.7 %all-to-all-start = ((bf16[256,16,1024]{2,0,1:T(8,128)(2,1)}), bf16[256,16,1024]{2,0,1:T(8,128)(2,1)}, u32[]{:S(2)}, u32[]{:S(2)}) async-start(bf16[256,16,1024]{2,0,1:T(8,128)(2,1)} %copy.27), calls=%async_computation | async-start | bytes 16777216 | tf_op jit(solution)/shard_map/all_to_all | solution.py:32
  174.9 92.2 %all-to-all-done = bf16[256,16,1024]{2,0,1:T(8,128)(2,1)} async-done(((bf16[256,16,1024]{2,0,1:T(8,128)(2,1)}), bf16[256,16,1024]{2,0,1:T(8,128)(2,1)}, u32[]{:S(2)}, u32[]{:S(2)}) %all-to-all-start) | async-done | bytes 8388640 | tf_op jit(solution)/shard_map/all_to_all | solution.py:32
  267.1 8.0 %copy.28 = bf16[4,256,4,1024]{3,1,0,2:T(8,128)(2,1)} copy(bf16[4,256,4,1024]{3,1,2,0:T(8,128)(2,1)} %bitcast.14) | data formatting | bytes 16777216 | tf_op jit(solution)/shard_map/all_to_all | solution.py:32
  275.1 111.2 %while.20 = (s32[]{:T(128)}, bf16[16,512,1024]{2,1,0:T(8,128)(2,1)}, bf16[16,512,1024]{2,1,0:T(8,128)(2,1)}, s32[16]{0:T(128)S(1)}, bf16[4,1024,1024]{2,1,0:T(8,128)(2,1)}, /*index=5*/s32[]{:T(128)}, s32[]{:T(128)}, s32[]{:T(128)}) while((s32[]{:T(128)}, bf16[16,512,1024]{2,1,0:T(8,128)(2,1)}, bf16[16,512,1024]{2,1,0:T(8,128)(2,1)}, ...), condition=%wide.region_1.2_spmd, body=%wide.region_0.1_spmd.sunk | while | flops 1074266112 | bytes 4195463 | solution.py:43
  275.1 0.7 dynamic_slice.48
  277.8 4.2 fusion.34
  282.0 0.7 dynamic_slice.48
  284.7 4.2 fusion.34
  288.9 0.7 dynamic_slice.48
  291.7 4.2 fusion.34
  295.9 0.7 dynamic_slice.48
  298.6 4.2 fusion.34
  302.8 0.7 dynamic_slice.48
  305.5 4.2 fusion.34
  309.7 0.7 dynamic_slice.48
  312.5 4.2 fusion.34
  316.7 0.7 dynamic_slice.48
  319.4 4.2 fusion.34
  323.6 0.7 dynamic_slice.48
  326.4 4.3 fusion.34
  330.6 0.7 dynamic_slice.48
  333.4 4.2 fusion.34
  337.6 0.7 dynamic_slice.48
  340.3 4.2 fusion.34
  344.5 0.7 dynamic_slice.48
  347.2 4.2 fusion.34
  351.4 0.7 dynamic_slice.48
  354.2 4.3 fusion.34
  358.5 0.7 dynamic_slice.48
  361.2 4.2 fusion.34
  365.4 0.7 dynamic_slice.48
  368.1 4.2 fusion.34
  372.3 0.7 dynamic_slice.48
  375.0 4.2 fusion.34
  379.2 0.7 dynamic_slice.48
  382.0 4.2 fusion.34
  386.2 1.3 fusion.26
  387.5 1.9 collective-permute-start
  389.4 2.6 collective-permute-start.1
  392.0 0.8 copy.23
  393.0 2.5 collective-permute-done
  395.5 4.4 collective-permute-done.1
  399.9 22.7 %pad_maximum_fusion = bf16[8704,1024]{1,0:T(8,128)(2,1)} fusion(bf16[256,1024]{1,0:T(8,128)(2,1)S(1)} %collective-permute-done.1, bf16[8192,1024]{1,0:T(8,128)(2,1)} %bitcast.67, bf16[256,1024]{1,0:T(8,128)(2,1)S(1)} %collective-permute-done), kind=kLoop, calls=%fused_computation.25 | loop fusion | flops 53477376 | bytes 35651584 | tf_op jit(solution)/shard_map/concatenate | solution.py:18
  422.6 122.7 %while.21 = (s32[]{:T(128)}, bf16[4,128,6,1024]{3,1,0,2:T(8,128)(2,1)}, bf16[4,128,6,24]{3,2,1,0:T(8,128)(2,1)S(1)}, s32[4,128,24]{2,1,0:T(8,128)S(1)}, bf16[8704,1024]{1,0:T(8,128)(2,1)}, /*index=5*/s32[]{:T(128)}) while((s32[]{:T(128)}, bf16[4,128,6,1024]{3,1,0,2:T(8,128)(2,1)}, bf16[4,128,6,24]{3,2,1,0:T(8,128)(2,1)S(1)}, ...), condition=%wide.region_3.4_spmd, body=%wide.region_2.3_spmd.sunk | while | flops 41711616 | bytes 23973456 | solution.py:57
  422.8 24.3 %gather_fusion = bf16[3072,1024]{1,0:T(8,128)(2,1)} fusion(bf16[8704,1024]{1,0:T(8,128)(2,1)} %get-tuple-element.185, s32[3072]{0:T(1024)S(1)} %broadcast_clamp_fusion.3), kind=kCustom, calls=%fused_computation.clone.1 | custom fusion | bytes 12595200 | tf_op jit(solution)/shard_map/while/body/eval_jaxpr/jit(_take)/gather | solution.py:51
  447.1 4.2 convert_bitcast_fusion.2
  451.3 2.0 copy_dynamic-update-slice_fusion.2
  453.4 24.3 %gather_fusion = bf16[3072,1024]{1,0:T(8,128)(2,1)} fusion(bf16[8704,1024]{1,0:T(8,128)(2,1)} %get-tuple-element.185, s32[3072]{0:T(1024)S(1)} %broadcast_clamp_fusion.3), kind=kCustom, calls=%fused_computation.clone.1 | custom fusion | bytes 12595200 | tf_op jit(solution)/shard_map/while/body/eval_jaxpr/jit(_take)/gather | solution.py:51
  477.7 4.2 convert_bitcast_fusion.2
  482.0 2.0 copy_dynamic-update-slice_fusion.2
  484.1 24.3 %gather_fusion = bf16[3072,1024]{1,0:T(8,128)(2,1)} fusion(bf16[8704,1024]{1,0:T(8,128)(2,1)} %get-tuple-element.185, s32[3072]{0:T(1024)S(1)} %broadcast_clamp_fusion.3), kind=kCustom, calls=%fused_computation.clone.1 | custom fusion | bytes 12595200 | tf_op jit(solution)/shard_map/while/body/eval_jaxpr/jit(_take)/gather | solution.py:51
  508.4 4.2 convert_bitcast_fusion.2
  512.6 2.0 copy_dynamic-update-slice_fusion.2
  514.8 24.3 %gather_fusion = bf16[3072,1024]{1,0:T(8,128)(2,1)} fusion(bf16[8704,1024]{1,0:T(8,128)(2,1)} %get-tuple-element.185, s32[3072]{0:T(1024)S(1)} %broadcast_clamp_fusion.3), kind=kCustom, calls=%fused_computation.clone.1 | custom fusion | bytes 12595200 | tf_op jit(solution)/shard_map/while/body/eval_jaxpr/jit(_take)/gather | solution.py:51
  539.1 4.2 convert_bitcast_fusion.2
  543.3 2.0 copy_dynamic-update-slice_fusion.2
  (29 shorter events, 0.7 us)
Async XLA Ops:
  6.5 151.4 %all-gather.2.cloned.1.call-start = ((), (), s32[]{:S(2)}) async-start(), calls=%async_computation.1 | async-start | bytes 9437184 | tf_op jit(solution)/shard_map/all_gather | solution.py:31
  169.2 97.9 %all-to-all-start = ((bf16[256,16,1024]{2,0,1:T(8,128)(2,1)}), bf16[256,16,1024]{2,0,1:T(8,128)(2,1)}, u32[]{:S(2)}, u32[]{:S(2)}) async-start(bf16[256,16,1024]{2,0,1:T(8,128)(2,1)} %copy.27), calls=%async_computation | async-start | bytes 16777216 | tf_op jit(solution)/shard_map/all_to_all | solution.py:32
  267.1 8.0 %copy-start.2 = (s32[16]{0:T(128)S(1)}, s32[16]{0:T(128)}, u32[]{:S(2)}) copy-start(s32[16]{0:T(128)} %param.13) | copy-start | bytes 196
  275.0 117.0 %copy-start = (bf16[512,6,24]{0,2,1:T(8,128)(2,1)S(1)}, bf16[512,6,24]{0,2,1:T(8,128)(2,1)}, u32[]{:S(2)}) copy-start(bf16[512,6,24]{0,2,1:T(8,128)(2,1)} %param.15) | copy-start | bytes 442372
  275.1 117.8 %copy-start.1 = (s32[512,24]{0,1:T(8,128)S(1)}, s32[512,24]{0,1:T(8,128)}, u32[]{:S(2)}) copy-start(s32[512,24]{0,1:T(8,128)} %param.14) | copy-start | bytes 147460
  387.5 8.0 %collective-permute-start = (bf16[256,1024]{1,0:T(8,128)(2,1)S(1)}, bf16[256,1024]{1,0:T(8,128)(2,1)S(1)}, u32[]{:S(2)}, u32[]{:S(2)}) collective-permute-start(bf16[256,1024]{1,0:T(8,128)(2,1)S(1)} %get-tuple-element.81), channel_id=1, source_target_pairs={{0,1},{1,2},{2,3},{3,4},{4,5},{5,6},{6,7},{8,9},{9,10},{10,11},{11... | collective-permute-start | bytes 1572872 | tf_op jit(solution)/shard_map/ppermute | solution.py:20
  389.4 10.5 %collective-permute-start.1 = (bf16[256,1024]{1,0:T(8,128)(2,1)S(1)}, bf16[256,1024]{1,0:T(8,128)(2,1)S(1)}, u32[]{:S(2)}, u32[]{:S(2)}) collective-permute-start(bf16[256,1024]{1,0:T(8,128)(2,1)S(1)} %get-tuple-element.82), channel_id=1, source_target_pairs={{1,0},{2,1},{3,2},{4,3},{5,4},{6,5},{7,6},{9,8},{10,9},{11,10},{12... | collective-permute-start | bytes 1572872 | tf_op jit(solution)/shard_map/ppermute | solution.py:22
Sparse Core Ops, SparseCore 0:
  73.3 84.5 all-gather.1
where the time goes:
time: 554 us; the launch traced here: 552 us
  local copies, waits for them, and re-layouts  201 us (36%)
  waiting for transfers between devices  184 us (33%)
  matrix products  84.3 us (15%)
  loops' own time  33.3 us (6%)
  other arithmetic  25.7 us (5%)
  between operations  13.5 us (2%)
  starting transfers between devices  10.2 us (2%)
    gather x4, local copies, waits for them, and re-layouts, one_part(): values = jnp.take(extended, link_rows, axis=0)  97.1 us
    all_to_all x1, waiting for transfers between devices, body(): lax.all_to_all(widened, 'group', split_axis=1, concat_axis=0, tiled=True)  92.2 us
    all_gather x1, waiting for transfers between devices, body(): widened = lax.all_gather(picked, 'row', axis=0, tiled=True)  84.7 us
    dot_general x16, matrix products, one_block(): lax.dot_general(matrix, sliced, (((1,), (1,)), ((), ())), preferred_eleme...  67.4 us
    gather x2, local copies, waits for them, and re-layouts, body(): picked = jnp.take(snapshots, bnd_index, axis=1)  61.9 us
    another operation x1, loops' own time, body(): interior = lax.map(one_block, (recovery, block_se))  33.2 us
    concatenate x1, other arithmetic, extended_2(): jnp.concatenate([lax.ppermute(tail, axis, [(i, (i + 1) % count) for i in...  22.7 us
    dot_general x4, matrix products, one_part(): jnp.einsum('eck,ekt->ect', mat_rows, values, preferred_element_type=jnp.f...  16.9 us
  transfers between devices with their start and end apart: 4, of which 4 were waited for; matrix products, arithmetic and copies ran while one was open for 0% of the time, Pallas kernels for 0%

commit v1 on v0

--- a/solution.py
+++ b/solution.py
@@ -3,10 +3,32 @@
 import jax.numpy as jnp
 from jax import lax
 from jax.sharding import PartitionSpec as P
+from jax.lax import axis_index, axis_size, ppermute
 
 HW = 256
 NC = 6
 NDOF = 24
+
+
+def settle_the_runs(xin):
+    ax_name = "row"
+    upper, kept_arr, current_arr = (axis_size(ax_name), axis_index(ax_name), xin.shape[0])
+    runs = [kk * upper if w == 0 else kk for w, kk in enumerate(xin.shape)]
+    view_out = lax.dynamic_update_slice_in_dim(
+        jnp.zeros(runs, xin.dtype), xin, kept_arr * current_arr, axis=0
+    )
+    r2 = tall = xin
+    for u in range(1, upper // 2 + 1):
+        r2 = ppermute(r2, ax_name, [(w, (w + 1) % upper) for w in range(upper)])
+        view_out = lax.dynamic_update_slice_in_dim(
+            view_out, r2, (kept_arr - u) % upper * current_arr, axis=0
+        )
+        if 2 * u < upper:
+            tall = ppermute(tall, ax_name, [(w, (w - 1) % upper) for w in range(upper)])
+            view_out = lax.dynamic_update_slice_in_dim(
+                view_out, tall, (kept_arr + u) % upper * current_arr, axis=0
+            )
+    return view_out
 
 
 def extended_2(cells, sides, width):
@@ -28,7 +50,7 @@
 
 def body(snapshots, bnd_index, recovery, block_se, connect, stress_mat):
     picked = jnp.take(snapshots, bnd_index, axis=1)
-    widened = lax.all_gather(picked, "row", axis=0, tiled=True)
+    widened = settle_the_runs(picked)
     arrived = lax.all_to_all(widened, "group", split_axis=1, concat_axis=0, tiled=True)
     bvals = jnp.transpose(arrived, (1, 0, 2))
 

time: 554 us -> 531 us (0.958)
  waiting for transfers between devices: 184 us -> 162 us
  between operations: 13.5 us -> 0.13 us
  starting transfers between devices: 10.2 us -> 22.5 us
  loops' own time: 33.3 us -> 26.5 us
    all_gather x1 -> x0, waiting for transfers between devices: 84.7 us -> none  [body(): widened = lax.all_gather(picked, 'row', axis=0, tiled=True)]
    ppermute x0 -> x7, waiting for transfers between devices: none -> 62.3 us  [the longest x4 54.9 us: settle_the_runs(): r2 = ppermute(r2, ax_name, [(w, (w + 1) % upper) for w in range(upper)])]
    dynamic_update_slice x0 -> x7, local copies, waits for them, and re-layouts: none -> 12.6 us  [the longest x4 6.86 us: settle_the_runs(): lax.dynamic_update_slice_in_dim(view_out, r2, (kept_arr - u) % upper * cu...]
    all_gather x1 -> x0, local copies, waits for them, and re-layouts: 11.3 us -> none  [body(): widened = lax.all_gather(picked, 'row', axis=0, tiled=True)]
    ppermute x0 -> x7, starting transfers between devices: none -> 10.2 us  [the longest x4 10.2 us: settle_the_runs(): r2 = ppermute(r2, ax_name, [(w, (w + 1) % upper) for w in range(upper)])]
    another operation x1, loops' own time: 33.2 us -> 26.4 us  [body(): interior = lax.map(one_block, (recovery, block_se))]
  transfers between devices with their start and end apart: 4 -> 10, of which waited for: 4 -> 10; matrix products, arithmetic and copies ran while one was open for 0% -> 2% of each run, Pallas kernels for 0% -> 0%
where the time goes in v1:
time: 531 us; the launch traced here: 526 us
  local copies, waits for them, and re-layouts  205 us (39%)
  waiting for transfers between devices  162 us (31%)
  matrix products  84.3 us (16%)
  loops' own time  26.5 us (5%)
  other arithmetic  25.9 us (5%)
  starting transfers between devices  22.5 us (4%)
    gather x4, local copies, waits for them, and re-layouts, one_part(): values = jnp.take(extended, link_rows, axis=0)  97.3 us
    all_to_all x1, waiting for transfers between devices, body(): lax.all_to_all(widened, 'group', split_axis=1, concat_axis=0, tiled=True)  91.8 us
    dot_general x16, matrix products, one_block(): lax.dot_general(matrix, sliced, (((1,), (1,)), ((), ())), preferred_eleme...  67.4 us
    gather x2, local copies, waits for them, and re-layouts, body(): picked = jnp.take(snapshots, bnd_index, axis=1)  61.4 us
    ppermute x4, waiting for transfers between devices, settle_the_runs(): r2 = ppermute(r2, ax_name, [(w, (w + 1) % upper) for w in range(upper)])  54.9 us
    another operation x1, loops' own time, body(): interior = lax.map(one_block, (recovery, block_se))  26.4 us
    concatenate x1, other arithmetic, extended_2(): jnp.concatenate([lax.ppermute(tail, axis, [(i, (i + 1) % count) for i in...  22.8 us
    dot_general x4, matrix products, one_part(): jnp.einsum('eck,ekt->ect', mat_rows, values, preferred_element_type=jnp.f...  16.9 us
  transfers between devices with their start and end apart: 10, of which 10 were waited for; matrix products, arithmetic and copies ran while one was open for 2% of the time, Pallas kernels for 0%

profile of v1, /device:TPU:1, one launch (start us, length us, event | category | flops | bytes accessed | tf_op | source)
XLA Modules:
  0.0 525.9 jit_solution(12030857701186819668)
XLA Ops:
  0.0 0.8 fusion.25
  0.8 0.9 compare_and_fusion.1
  1.7 1.9 copy.18
  3.7 57.9 %gather_fusion.1 = bf16[16384,32]{1,0:T(8,128)(2,1)} fusion(bf16[32,8192]{0,1:T(8,128)(2,1)S(1)} %copy.18, s32[16384]{0:T(1024)S(1)} %broadcast_clamp_fusion.1), kind=kCustom, calls=%fused_computation.1 | custom fusion | bytes 2162688 | tf_op jit(solution)/shard_map/jit(_take)/gather | solution.py:52
  61.6 3.5 copy.19
  65.1 4.3 broadcast_in_dim.41
  69.4 1.3 constant_dynamic-update-slice_fusion.7
  70.7 2.7 collective-permute-start
  73.4 20.9 %collective-permute-done = bf16[32,16,1024]{2,0,1:T(8,128)(2,1)S(1)} collective-permute-done((bf16[32,16,1024]{2,0,1:T(8,128)(2,1)S(1)}, bf16[32,16,1024]{2,0,1:T(8,128)(2,1)S(1)}, u32[]{:S(2)}, u32[]{:S(2)}) %collective-permute-start) | collective-permute-done | bytes 1048608 | tf_op jit(solution)/shard_map/ppermute | solution.py:22
  94.3 2.5 collective-permute-start.2
  96.8 1.5 collective-permute-done.1
  98.3 17.4 %collective-permute-done.2 = bf16[32,16,1024]{2,0,1:T(8,128)(2,1)S(1)} collective-permute-done((bf16[32,16,1024]{2,0,1:T(8,128)(2,1)S(1)}, bf16[32,16,1024]{2,0,1:T(8,128)(2,1)S(1)}, u32[]{:S(2)}, u32[]{:S(2)}) %collective-permute-start.2) | collective-permute-done | bytes 1048608 | tf_op jit(solution)/shard_map/ppermute | solution.py:22
  115.7 2.5 collective-permute-start.4
  118.2 4.9 collective-permute-done.3
  123.1 13.0 %collective-permute-done.4 = bf16[32,16,1024]{2,0,1:T(8,128)(2,1)S(1)} collective-permute-done((bf16[32,16,1024]{2,0,1:T(8,128)(2,1)S(1)}, bf16[32,16,1024]{2,0,1:T(8,128)(2,1)S(1)}, u32[]{:S(2)}, u32[]{:S(2)}) %collective-permute-start.4) | collective-permute-done | bytes 1048608 | tf_op jit(solution)/shard_map/ppermute | solution.py:22
  136.0 2.5 collective-permute-start.6
  138.5 1.1 constant_dynamic-update-slice_fusion.6
  139.7 1.1 constant_dynamic-update-slice_fusion.5
  140.8 2.3 constant_dynamic-update-slice_fusion.4
  143.2 2.3 constant_dynamic-update-slice_fusion.3
  145.4 1.1 constant_dynamic-update-slice_fusion.2
  146.5 1.0 collective-permute-done.5
  147.5 2.3 constant_dynamic-update-slice_fusion.1
  149.8 3.7 collective-permute-done.6
  153.5 2.3 constant_dynamic-update-slice_fusion
  155.8 5.7 %all-to-all-start = ((bf16[256,16,1024]{2,0,1:T(8,128)(2,1)}), bf16[256,16,1024]{2,0,1:T(8,128)(2,1)}, u32[]{:S(2)}, u32[]{:S(2)}) async-start(bf16[256,16,1024]{2,0,1:T(8,128)(2,1)} %constant_dynamic-update-slice_fusion), calls=%async_computation | async-start | bytes 16777216 | tf_op jit(solution)/shard_map/all_to_all | solution.py:54
  161.5 91.8 %all-to-all-done = bf16[256,16,1024]{2,0,1:T(8,128)(2,1)} async-done(((bf16[256,16,1024]{2,0,1:T(8,128)(2,1)}), bf16[256,16,1024]{2,0,1:T(8,128)(2,1)}, u32[]{:S(2)}, u32[]{:S(2)}) %all-to-all-start) | async-done | bytes 8388640 | tf_op jit(solution)/shard_map/all_to_all | solution.py:54
  253.3 8.0 %copy.20 = bf16[4,256,4,1024]{3,1,0,2:T(8,128)(2,1)} copy(bf16[4,256,4,1024]{3,1,2,0:T(8,128)(2,1)} %bitcast.14) | data formatting | bytes 16777216 | tf_op jit(solution)/shard_map/all_to_all | solution.py:54
  261.3 102.7 %while.20 = (s32[]{:T(128)}, bf16[16,512,1024]{2,1,0:T(8,128)(2,1)}, bf16[16,512,1024]{2,1,0:T(8,128)(2,1)}, s32[16]{0:T(128)S(1)}, bf16[4,1024,1024]{2,1,0:T(8,128)(2,1)}, /*index=5*/s32[]{:T(128)}, s32[]{:T(128)}, s32[]{:T(128)}) while((s32[]{:T(128)}, bf16[16,512,1024]{2,1,0:T(8,128)(2,1)}, bf16[16,512,1024]{2,1,0:T(8,128)(2,1)}, ...), condition=%wide.region_1.2_spmd, body=%wide.region_0.1_spmd.sunk | while | flops 1074266112 | bytes 4195463 | solution.py:65
  263.5 4.2 fusion.34
  269.9 4.2 fusion.34
  276.3 4.2 fusion.34
  282.7 4.2 fusion.34
  289.1 4.2 fusion.34
  295.5 4.2 fusion.34
  301.9 4.3 fusion.34
  308.4 4.3 fusion.34
  314.9 4.2 fusion.34
  321.3 4.2 fusion.34
  327.7 4.2 fusion.34
  334.1 4.2 fusion.34
  340.6 4.2 fusion.34
  346.9 4.2 fusion.34
  353.3 4.2 fusion.34
  359.8 4.2 fusion.34
  364.0 1.3 fusion.26
  365.3 4.6 collective-permute-start.7
  369.8 2.1 collective-permute-start.8
  372.9 3.1 collective-permute-done.7
  375.9 4.4 collective-permute-done.8
  380.3 22.8 %pad_maximum_fusion = bf16[8704,1024]{1,0:T(8,128)(2,1)} fusion(bf16[256,1024]{1,0:T(8,128)(2,1)S(1)} %collective-permute-done.8, bf16[8192,1024]{1,0:T(8,128)(2,1)} %bitcast.68, bf16[256,1024]{1,0:T(8,128)(2,1)S(1)} %collective-permute-done.7), kind=kLoop, calls=%fused_computation.25 | loop fusion | flops 53477376 | bytes 35651584 | tf_op jit(solution)/shard_map/concatenate | solution.py:40
  403.1 122.8 %while.21 = (s32[]{:T(128)}, bf16[4,128,6,1024]{3,1,0,2:T(8,128)(2,1)}, bf16[4,128,6,24]{3,2,1,0:T(8,128)(2,1)S(1)}, s32[4,128,24]{2,1,0:T(8,128)S(1)}, bf16[8704,1024]{1,0:T(8,128)(2,1)}, /*index=5*/s32[]{:T(128)}) while((s32[]{:T(128)}, bf16[4,128,6,1024]{3,1,0,2:T(8,128)(2,1)}, bf16[4,128,6,24]{3,2,1,0:T(8,128)(2,1)S(1)}, ...), condition=%wide.region_3.4_spmd, body=%wide.region_2.3_spmd.sunk | while | flops 41711616 | bytes 23973456 | solution.py:79
  403.2 24.3 %gather_fusion = bf16[3072,1024]{1,0:T(8,128)(2,1)} fusion(bf16[8704,1024]{1,0:T(8,128)(2,1)} %get-tuple-element.187, s32[3072]{0:T(1024)S(1)} %broadcast_clamp_fusion.3), kind=kCustom, calls=%fused_computation.clone.1 | custom fusion | bytes 12595200 | tf_op jit(solution)/shard_map/while/body/eval_jaxpr/jit(_take)/gather | solution.py:73
  427.6 4.2 convert_bitcast_fusion.2
  431.8 2.0 copy_dynamic-update-slice_fusion.2
  433.9 24.3 %gather_fusion = bf16[3072,1024]{1,0:T(8,128)(2,1)} fusion(bf16[8704,1024]{1,0:T(8,128)(2,1)} %get-tuple-element.187, s32[3072]{0:T(1024)S(1)} %broadcast_clamp_fusion.3), kind=kCustom, calls=%fused_computation.clone.1 | custom fusion | bytes 12595200 | tf_op jit(solution)/shard_map/while/body/eval_jaxpr/jit(_take)/gather | solution.py:73
  458.3 4.2 convert_bitcast_fusion.2
  462.5 2.0 copy_dynamic-update-slice_fusion.2
  464.6 24.3 %gather_fusion = bf16[3072,1024]{1,0:T(8,128)(2,1)} fusion(bf16[8704,1024]{1,0:T(8,128)(2,1)} %get-tuple-element.187, s32[3072]{0:T(1024)S(1)} %broadcast_clamp_fusion.3), kind=kCustom, calls=%fused_computation.clone.1 | custom fusion | bytes 12595200 | tf_op jit(solution)/shard_map/while/body/eval_jaxpr/jit(_take)/gather | solution.py:73
  489.0 4.2 convert_bitcast_fusion.2
  493.2 2.0 copy_dynamic-update-slice_fusion.2
  495.3 24.3 %gather_fusion = bf16[3072,1024]{1,0:T(8,128)(2,1)} fusion(bf16[8704,1024]{1,0:T(8,128)(2,1)} %get-tuple-element.187, s32[3072]{0:T(1024)S(1)} %broadcast_clamp_fusion.3), kind=kCustom, calls=%fused_computation.clone.1 | custom fusion | bytes 12595200 | tf_op jit(solution)/shard_map/while/body/eval_jaxpr/jit(_take)/gather | solution.py:73
  519.6 4.2 convert_bitcast_fusion.2
  523.9 2.0 copy_dynamic-update-slice_fusion.2
  (49 shorter events, 10.3 us)
Async XLA Ops:
  70.7 23.6 %collective-permute-start = (bf16[32,16,1024]{2,0,1:T(8,128)(2,1)S(1)}, bf16[32,16,1024]{2,0,1:T(8,128)(2,1)S(1)}, u32[]{:S(2)}, u32[]{:S(2)}) collective-permute-start(bf16[32,16,1024]{2,0,1:T(8,128)(2,1)S(1)} %get-tuple-element.82), channel_id=1, source_target_pairs={{0,1},{1,2},{2,3},{3,4},{4,5},{5,6},{6,7},{7,0},{8,9},{9,10},{10,1... | collective-permute-start | bytes 3145736 | tf_op jit(solution)/shard_map/ppermute | solution.py:22
  73.4 24.9 %collective-permute-start.1 = (bf16[32,16,1024]{2,0,1:T(8,128)(2,1)S(1)}, bf16[32,16,1024]{2,0,1:T(8,128)(2,1)S(1)}, u32[]{:S(2)}, u32[]{:S(2)}) collective-permute-start(bf16[32,16,1024]{2,0,1:T(8,128)(2,1)S(1)} %get-tuple-element.82), channel_id=1, source_target_pairs={{0,7},{1,0},{2,1},{3,2},{4,3},{5,4},{6,5},{7,6},{8,15},{9,8},{10,9... | collective-permute-start | bytes 3145736 | tf_op jit(solution)/shard_map/ppermute | solution.py:27
  94.3 21.4 %collective-permute-start.2 = (bf16[32,16,1024]{2,0,1:T(8,128)(2,1)S(1)}, bf16[32,16,1024]{2,0,1:T(8,128)(2,1)S(1)}, u32[]{:S(2)}, u32[]{:S(2)}) collective-permute-start(bf16[32,16,1024]{2,0,1:T(8,128)(2,1)S(1)} %collective-permute-done), channel_id=1, source_target_pairs={{0,1},{1,2},{2,3},{3,4},{4,5},{5,6},{6,7},{7,0},{8,9},{9,10},{10,1... | collective-permute-start | bytes 3145736 | tf_op jit(solution)/shard_map/ppermute | solution.py:22
  98.3 24.8 %collective-permute-start.3 = (bf16[32,16,1024]{2,0,1:T(8,128)(2,1)S(1)}, bf16[32,16,1024]{2,0,1:T(8,128)(2,1)}, u32[]{:S(2)}, u32[]{:S(2)}) collective-permute-start(bf16[32,16,1024]{2,0,1:T(8,128)(2,1)S(1)} %collective-permute-done.1), channel_id=1, source_target_pairs={{0,7},{1,0},{2,1},{3,2},{4,3},{5,4},{6,5},{7,6},{8,15},{9,8},{10,9... | collective-permute-start | bytes 3145736 | tf_op jit(solution)/shard_map/ppermute | solution.py:27
  115.7 20.4 %copy-start = (bf16[32,16,1024]{2,0,1:T(8,128)(2,1)}, bf16[32,16,1024]{2,0,1:T(8,128)(2,1)S(1)}, u32[]{:S(2)}) copy-start(bf16[32,16,1024]{2,0,1:T(8,128)(2,1)S(1)} %collective-permute-done.2) | copy-start | bytes 3145732
  115.7 20.4 %collective-permute-start.4 = (bf16[32,16,1024]{2,0,1:T(8,128)(2,1)S(1)}, bf16[32,16,1024]{2,0,1:T(8,128)(2,1)S(1)}, u32[]{:S(2)}, u32[]{:S(2)}) collective-permute-start(bf16[32,16,1024]{2,0,1:T(8,128)(2,1)S(1)} %collective-permute-done.2), channel_id=1, source_target_pairs={{0,1},{1,2},{2,3},{3,4},{4,5},{5,6},{6,7},{7,0},{8,9},{9,10},{10,1... | collective-permute-start | bytes 3145736 | tf_op jit(solution)/shard_map/ppermute | solution.py:22
  123.1 24.4 %collective-permute-start.5 = (bf16[32,16,1024]{2,0,1:T(8,128)(2,1)}, bf16[32,16,1024]{2,0,1:T(8,128)(2,1)}, u32[]{:S(2)}, u32[]{:S(2)}) collective-permute-start(bf16[32,16,1024]{2,0,1:T(8,128)(2,1)} %collective-permute-done.3), channel_id=1, source_target_pairs={{0,7},{1,0},{2,1},{3,2},{4,3},{5,4},{6,5},{7,6},{8,15},{9,8},{10,9... | collective-permute-start | bytes 3145736 | tf_op jit(solution)/shard_map/ppermute | solution.py:27
  136.0 17.4 %collective-permute-start.6 = (bf16[32,16,1024]{2,0,1:T(8,128)(2,1)S(1)}, bf16[32,16,1024]{2,0,1:T(8,128)(2,1)}, u32[]{:S(2)}, u32[]{:S(2)}) collective-permute-start(bf16[32,16,1024]{2,0,1:T(8,128)(2,1)S(1)} %collective-permute-done.4), channel_id=1, source_target_pairs={{0,1},{1,2},{2,3},{3,4},{4,5},{5,6},{6,7},{7,0},{8,9},{9,10},{10,1... | collective-permute-start | bytes 3145736 | tf_op jit(solution)/shard_map/ppermute | solution.py:22
  155.8 97.5 %all-to-all-start = ((bf16[256,16,1024]{2,0,1:T(8,128)(2,1)}), bf16[256,16,1024]{2,0,1:T(8,128)(2,1)}, u32[]{:S(2)}, u32[]{:S(2)}) async-start(bf16[256,16,1024]{2,0,1:T(8,128)(2,1)} %constant_dynamic-update-slice_fusion), calls=%async_computation | async-start | bytes 16777216 | tf_op jit(solution)/shard_map/all_to_all | solution.py:54
  253.3 8.0 %copy-start.3 = (s32[16]{0:T(128)S(1)}, s32[16]{0:T(128)}, u32[]{:S(2)}) copy-start(s32[16]{0:T(128)} %param.13) | copy-start | bytes 196
  261.3 110.7 %copy-start.1 = (bf16[512,6,24]{0,2,1:T(8,128)(2,1)S(1)}, bf16[512,6,24]{0,2,1:T(8,128)(2,1)}, u32[]{:S(2)}) copy-start(bf16[512,6,24]{0,2,1:T(8,128)(2,1)} %param.15) | copy-start | bytes 442372
  261.3 111.5 %copy-start.2 = (s32[512,24]{0,1:T(8,128)S(1)}, s32[512,24]{0,1:T(8,128)}, u32[]{:S(2)}) copy-start(s32[512,24]{0,1:T(8,128)} %param.14) | copy-start | bytes 147460
  365.3 10.7 %collective-permute-start.7 = (bf16[256,1024]{1,0:T(8,128)(2,1)S(1)}, bf16[256,1024]{1,0:T(8,128)(2,1)S(1)}, u32[]{:S(2)}, u32[]{:S(2)}) collective-permute-start(bf16[256,1024]{1,0:T(8,128)(2,1)S(1)} %get-tuple-element.83), channel_id=1, source_target_pairs={{0,1},{1,2},{2,3},{3,4},{4,5},{5,6},{6,7},{8,9},{9,10},{10,11},{11... | collective-permute-start | bytes 1572872 | tf_op jit(solution)/shard_map/ppermute | solution.py:42
  369.8 10.5 %collective-permute-start.8 = (bf16[256,1024]{1,0:T(8,128)(2,1)S(1)}, bf16[256,1024]{1,0:T(8,128)(2,1)S(1)}, u32[]{:S(2)}, u32[]{:S(2)}) collective-permute-start(bf16[256,1024]{1,0:T(8,128)(2,1)S(1)} %get-tuple-element.84), channel_id=1, source_target_pairs={{1,0},{2,1},{3,2},{4,3},{5,4},{6,5},{7,6},{9,8},{10,9},{11,10},{12... | collective-permute-start | bytes 1572872 | tf_op jit(solution)/shard_map/ppermute | solution.py:44
